TPU v7x, 256 devices: a whole 4x4x8 slice. The times are simulated.
256 devices in a mesh: rows: 64 (over y, z, core), cols: 4 (over x).
Axes of the slice: x: 4, y: 4, z: 8, core: 2. Of those that a mesh axis runs over, the one named last changes fastest.
Arguments:
- residual_block: float32 [524288, 64], P('rows', 'cols'), may hold values from -6 to 6
- basis: bfloat16 [524288, 64], P('rows', 'cols'), may hold values from -0.0078125 to 0.0078125
- fine_tiles: bfloat16 [4096, 4, 128, 128], P('rows')
- fine_index: int32 [4096, 4], P('rows'), may hold values from 0 to 4095, as said below
- mid_tiles: bfloat16 [512, 3, 128, 128], P('rows')
- fine_owner: int32 [524288], P('rows'), may hold values from 0 to 65535, as said below
- mid_owner: int32 [65536], P('rows'), may hold values from 0 to 8191, as said below
- coarse_inverse: float32 [8192, 8192], P('rows'), as said below
Outputs:
- directions: float32 [524288, 64], P('rows', 'cols')
- gram: float32 [64, 64], P(None, 'cols')
Inputs may be any that keep to these rules, and one draw needn't show every extreme that they name: `fine_index`: slot 0 of block row g names g itself; every block named in a block row of partition p (block rows p*64 to p*64 + 63) belongs to partition p - 1, p or p + 1. `fine_owner`: the fine vertices of partition p map to level-one rows p*1024 to p*1024 + 1023; every level-one row receives exactly 8 vertices. `mid_owner`: the level-one rows of partitions 2q and 2q + 1 map to level-two rows 2q*128 to 2q*128 + 2*128 - 1; every level-two row receives exactly 8 level-one rows. coarse_inverse is symmetric.
All inputs are finite; a program needn't handle non-finite values.
Results may differ from a plain program's by a relative error of at most 0.013.
Values may be sent and summed in bfloat16 or wider, within the bound.
A program may use at most 64 MiB of HBM per device.

v0:
```python
import jax
import jax.numpy as jnp
from jax import lax
from jax.sharding import PartitionSpec as P

DAMPING = 0.6666666666666666


def with_halo(array, sides, width):
    for axis, dim in sides:
        peers, length = (lax.axis_size(axis), array.shape[dim])
        up = [(i, (i + 1) % peers) for i in range(peers - 1)]
        down = [(j, i) for i, j in up]
        last = lax.slice_in_dim(array, length - width, length, axis=dim)
        leading = lax.slice_in_dim(array, 0, width, axis=dim)
        before = lax.ppermute(last, axis, up)
        after = lax.ppermute(leading, axis, down)
        array = jnp.concatenate([before, array, after], axis=dim)
    return array


def swapped(value, axis, apart):
    mask = 2**apart
    pairs = [(source, source ^ mask) for source in range(lax.axis_size(axis))]
    return lax.ppermute(value, axis, pairs)


def fine_apply(vector, matrix, window_index):
    extent = matrix.shape[2]
    packed = vector.astype(jnp.bfloat16).reshape(-1, extent, vector.shape[1])
    window = with_halo(packed, (("rows", 0),), packed.shape[0])
    picked = window[window_index]
    product = jnp.einsum("bkij,bkjc->bic", matrix, picked, preferred_element_type=jnp.float32)
    return product.reshape(vector.shape)


def mid_apply(vector, matrix):
    blocks = matrix.shape[0]
    extent = matrix.shape[2]
    packed = vector.astype(jnp.bfloat16).reshape(blocks, extent, vector.shape[1])
    window = with_halo(packed, (("rows", 0),), 1)
    product = jnp.einsum(
        "bij,bjc->bic", matrix[:, 0], window[:-2], preferred_element_type=jnp.float32
    )
    product = product + jnp.einsum(
        "bij,bjc->bic", matrix[:, 1], window[1:-1], preferred_element_type=jnp.float32
    )
    product = product + jnp.einsum(
        "bij,bjc->bic", matrix[:, 2], window[2:], preferred_element_type=jnp.float32
    )
    return product.reshape(vector.shape)


def on_device(
    residual_block, basis, fine_tiles, fine_index, mid_tiles, fine_owner, mid_owner, coarse_inverse
):
    device = lax.axis_index("rows")
    blocks = fine_tiles.shape[0]
    mid_count = mid_tiles.shape[0] * mid_tiles.shape[2]
    coarse_count = coarse_inverse.shape[0]
    col_width = residual_block.shape[1]
    parity = device % 2
    window_index = fine_index - (device - 1) * blocks
    fine_local = fine_owner - device * mid_count
    mid_local = mid_owner - (device - parity) * coarse_count
    fine_inv = 1.0 / jnp.diagonal(fine_tiles[:, 0], axis1=1, axis2=2).astype(jnp.float32).reshape(
        -1, 1
    )
    mid_inv = 1.0 / jnp.diagonal(mid_tiles[:, 1], axis1=1, axis2=2).astype(jnp.float32).reshape(
        -1, 1
    )
    fine_x = DAMPING * fine_inv * residual_block
    fine_x = fine_x + DAMPING * fine_inv * (
        residual_block - fine_apply(fine_x, fine_tiles, window_index)
    )
    fine_res = residual_block - fine_apply(fine_x, fine_tiles, window_index)
    partial_mid = jax.ops.segment_sum(fine_res, fine_local, num_segments=mid_count)
    mid_x = DAMPING * mid_inv * partial_mid
    mid_x = mid_x + DAMPING * mid_inv * (partial_mid - mid_apply(mid_x, mid_tiles))
    mid_res = partial_mid - mid_apply(mid_x, mid_tiles)
    partial_value = jax.ops.segment_sum(mid_res, mid_local, num_segments=2 * coarse_count)
    halves = partial_value.reshape(2, coarse_count, col_width)
    own_half = jnp.where(parity == 0, halves[0], halves[1])
    other_half = jnp.where(parity == 0, halves[1], halves[0])
    coarse_rhs = own_half + swapped(other_half, "rows", 0)
    coarse_fix = jnp.dot(
        coarse_inverse,
        lax.all_gather(coarse_rhs, "rows", axis=0, tiled=True),
        precision=lax.Precision.HIGHEST,
        preferred_element_type=jnp.float32,
    )
    partner_fix = swapped(coarse_fix, "rows", 0)
    pair_values = jnp.where(
        parity == 0,
        jnp.concatenate([coarse_fix, partner_fix], axis=0),
        jnp.concatenate([partner_fix, coarse_fix], axis=0),
    )
    mid_x = mid_x + pair_values[mid_local]
    mid_x = mid_x + DAMPING * mid_inv * (partial_mid - mid_apply(mid_x, mid_tiles))
    fine_x = fine_x + mid_x[fine_local]
    finished = fine_x + DAMPING * fine_inv * (
        residual_block - fine_apply(fine_x, fine_tiles, window_index)
    )
    rounded = finished.astype(jnp.bfloat16)
    partial_gram = lax.dot_general(
        lax.all_gather(basis, "cols", axis=1, tiled=True),
        rounded,
        (((0,), (0,)), ((), ())),
        preferred_element_type=jnp.float32,
    )
    gram = lax.psum(partial_gram, "rows")
    return (finished, gram)


def solution(mesh):
    in_specs = (
        P("rows", "cols"),
        P("rows", "cols"),
        P("rows", None, None, None),
        P("rows", None),
        P("rows", None, None, None),
        P("rows"),
        P("rows"),
        P("rows", None),
    )
    out_specs = (P("rows", "cols"), P(None, "cols"))
    return jax.shard_map(
        on_device, mesh=mesh, in_specs=in_specs, out_specs=out_specs, check_vma=False
    )
```

profile of v0, /device:TPU:4, one launch (start us, length us, event | category | flops | bytes accessed | tf_op | source)
XLA Modules:
  0.0 407.9 jit_solution(2754003155523653004)
XLA Ops:
  8.8 3.9 copy.204
  12.7 1.9 gather_fusion
  19.1 3.1 copy.166
  25.2 5.7 %convolution_bitcast_fusion.2 = f32[64,2,8,128]{3,2,1,0:T(8,128)S(1)} fusion(bf16[64,4,128,16]{2,3,1,0:T(8,128)(2,1)S(1)} %bitcast.177, bf16[64,4,128,128]{3,2,1,0:T(8,128)(2,1)} %param.10), kind=kOutput, calls=%fused_computation.11 | convolution fusion | flops 134217728 | bytes 9961472 | tf_op jit(solution)/shard_map/bkij,bkjc->bic/dot_general | solution.py:33
  31.0 4.7 %collective-permute-start.2 = (bf16[64,128,16]{1,2,0:T(8,128)(2,1)S(1)}, bf16[64,128,16]{1,2,0:T(8,128)(2,1)S(1)}, u32[]{:S(2)}, u32[]{:S(2)}) collective-permute-start(bf16[64,128,16]{1,2,0:T(8,128)(2,1)S(1)} %copy_bitcast_fusion.1), channel_id=1, source_target_pairs={{0,4},{4,8},{8,12},{12,16},{16,20},{20,24},{24,28},{28,32},{32,36}... | collective-permute-start | bytes 786440 | tf_op jit(solution)/shard_map/ppermute | solution.py:16
  37.1 3.3 collective-permute-done.3
  41.3 5.7 %convolution_bitcast_fusion.1 = f32[64,2,8,128]{3,2,1,0:T(8,128)S(1)} fusion(bf16[64,4,128,16]{2,3,1,0:T(8,128)(2,1)S(1)} %bitcast.178, bf16[64,4,128,128]{3,2,1,0:T(8,128)(2,1)} %param.10), kind=kOutput, calls=%fused_computation.10 | convolution fusion | flops 134217728 | bytes 9961472 | tf_op jit(solution)/shard_map/bkij,bkjc->bic/dot_general | solution.py:33
  47.1 2.6 copy.172
  49.7 44.4 %scatter_custom_fusion = f32[1024,16]{1,0:T(8,128)S(1)} fusion(s32[8192]{0:T(1024)S(1)} %get-tuple-element.11, f32[8192,16]{1,0:T(8,128)} %copy.172, f32[]{:T(128)} %constant.25.clone.1), kind=kCustom, calls=%fused_computation.51 | custom fusion | flops 131072 | bytes 66048 | tf_op jit(solution)/shard_map/scatter-add | solution.py:77
  95.9 7.3 %collective-permute-start.4 = (bf16[1,128,16]{1,2,0:T(8,128)(2,1)S(1)}, bf16[1,128,16]{1,2,0:T(8,128)(2,1)S(1)}, u32[]{:S(2)}, u32[]{:S(2)}) collective-permute-start(bf16[1,128,16]{1,2,0:T(8,128)(2,1)S(1)} %get-tuple-element.18), channel_id=1, source_target_pairs={{0,4},{4,8},{8,12},{12,16},{16,20},{20,24},{24,28},{28,32},{32,36}... | collective-permute-start | bytes 12296 | tf_op jit(solution)/shard_map/ppermute | solution.py:16
  105.8 4.2 %collective-permute-start.6 = (bf16[1,128,16]{1,2,0:T(8,128)(2,1)S(1)}, bf16[1,128,16]{1,2,0:T(8,128)(2,1)S(1)}, u32[]{:S(2)}, u32[]{:S(2)}) collective-permute-start(bf16[1,128,16]{1,2,0:T(8,128)(2,1)S(1)} %get-tuple-element.16), channel_id=1, source_target_pairs={{0,4},{4,8},{8,12},{12,16},{16,20},{20,24},{24,28},{28,32},{32,36}... | collective-permute-start | bytes 12296 | tf_op jit(solution)/shard_map/ppermute | solution.py:16
  112.2 6.4 %scatter_custom_fusion.1 = f32[256,16]{1,0:T(8,128)S(1)} fusion(s32[1024]{0:T(1024)S(1)} %get-tuple-element.13, f32[1024,16]{1,0:T(8,128)} %bitcast_subtract_fusion.3, f32[]{:T(128)} %constant.25.clone.1), kind=kCustom, calls=%fused_computation.70 | custom fusion | flops 16384 | bytes 16896 | tf_op jit(solution)/shard_map/scatter-add | solution.py:81
  118.6 2.5 collective-permute-start.8
  122.0 65.2 %all_gather.6 = f32[8192,16]{1,0:T(8,128)S(1)} all-gather(f32[128,16]{1,0:T(8,128)S(1)} %select_add_fusion), channel_id=1, replica_groups=mesh['rows'=64,'cols'=4] {'rows'}, dimensions={0}, use_global_device_ids=true | all-gather | bytes 532480 | tf_op jit(solution)/shard_map/all_gather | solution.py:88
  187.2 6.6 %convolution_bitcast_fusion.4 = f32[128,16]{0,1:T(8,128)S(1)} fusion(f32[8192,16]{1,0:T(8,128)S(1)} %all_gather.6, f32[128,8192]{1,0:T(8,128)S(1)} %copy-done.2), kind=kOutput, calls=%fused_computation.22 | convolution fusion | flops 201326592 | bytes 4726784 | tf_op jit(solution)/shard_map/dot_general | solution.py:86
  195.1 2.8 gather_fusion.4
  199.7 3.0 collective-permute-start.10
  204.0 27.9 %gather_fusion.5 = f32[8192,16]{1,0:T(8,128)} fusion(f32[1024,16]{1,0:T(8,128)S(1)} %copy.193, s32[8192]{0:T(1024)S(1)} %get-tuple-element.10), kind=kCustom, calls=%fused_computation.5 | custom fusion | bytes 1081344 | tf_op jit(solution)/shard_map/gather | solution.py:100
  231.9 2.8 copy.194
  234.8 3.4 collective-permute-start.12
  239.6 3.9 collective-permute-done.13
  244.4 5.7 %convolution_bitcast_fusion = f32[64,2,8,128]{3,2,1,0:T(8,128)S(1)} fusion(bf16[64,4,128,16]{2,3,1,0:T(8,128)(2,1)S(1)} %bitcast.176, bf16[64,4,128,128]{3,2,1,0:T(8,128)(2,1)} %param.10), kind=kOutput, calls=%fused_computation.9 | convolution fusion | flops 134217728 | bytes 9961472 | tf_op jit(solution)/shard_map/bkij,bkjc->bic/dot_general | solution.py:33
  250.3 18.4 %all-gather.2.cloned.1.call-done = bf16[8192,64]{0,1:T(8,128)(2,1)} async-done(((bf16[8192,16]{0,1:T(8,128)(2,1)}), bf16[8192,64]{0,1:T(8,128)(2,1)}) %all-gather.2.cloned.1.call-update) | async-done | bytes 1048592 | tf_op jit(solution)/shard_map/all_gather | solution.py:106
  270.3 130.8 %psum.7 = f32[64,16]{0,1:T(8,128)} all-reduce(f32[64,16]{0,1:T(8,128)S(1)} %convolution_bitcast_fusion.3), channel_id=1, replica_groups=mesh['rows'=64,'cols'=4] {'rows'}, use_global_device_ids=true, to_apply=%region_2.3 | all-reduce | flops 1024 | bytes 8192 | tf_op jit(solution)/shard_map/psum | solution.py:111
  (91 shorter events, 27.2 us)
Async XLA Ops:
  7.2 1.6 slice-start
  7.2 261.5 %all-gather.2.cloned.1.call-start = ((), (), s32[]{:S(2)}) async-start(), calls=%async_computation | async-start | bytes 1310720 | tf_op jit(solution)/shard_map/all_gather | solution.py:106
  8.8 6.0 %copy-start = (f32[8192,16]{0,1:T(8,128)S(1)}, f32[8192,16]{0,1:T(8,128)}, u32[]{:S(2)}) copy-start(f32[8192,16]{0,1:T(8,128)} %param.8) | copy-start | bytes 1572868
  8.8 9.1 %copy-start.6 = (s32[64,4]{0,1:T(4,128)S(1)}, s32[64,4]{0,1:T(4,128)}, u32[]{:S(2)}) copy-start(s32[64,4]{0,1:T(4,128)} %param.11) | copy-start | bytes 3076
  12.7 11.5 %copy-start.5 = (s32[1024]{0:T(1024)S(1)}, s32[1024]{0:T(1024)}, u32[]{:S(2)}) copy-start(s32[1024]{0:T(1024)} %param.14) | copy-start | bytes 12292
  14.8 9.4 %collective-permute-start = (bf16[64,128,16]{1,2,0:T(8,128)(2,1)S(1)}, bf16[64,128,16]{1,2,0:T(8,128)(2,1)S(1)}, u32[]{:S(2)}, u32[]{:S(2)}) collective-permute-start(bf16[64,128,16]{1,2,0:T(8,128)(2,1)S(1)} %copy_bitcast_fusion.2), channel_id=1, source_target_pairs={{0,4},{4,8},{8,12},{12,16},{16,20},{20,24},{24,28},{28,32},{32,36}... | collective-permute-start | bytes 786440 | tf_op jit(solution)/shard_map/ppermute | solution.py:16
  16.5 7.7 %collective-permute-start.1 = (bf16[64,128,16]{1,2,0:T(8,128)(2,1)S(1)}, bf16[64,128,16]{1,2,0:T(8,128)(2,1)S(1)}, u32[]{:S(2)}, u32[]{:S(2)}) collective-permute-start(bf16[64,128,16]{1,2,0:T(8,128)(2,1)S(1)} %copy_bitcast_fusion.2), channel_id=1, source_target_pairs={{4,0},{8,4},{12,8},{16,12},{20,16},{24,20},{28,24},{32,28},{36,32}... | collective-permute-start | bytes 786440 | tf_op jit(solution)/shard_map/ppermute | solution.py:17
  25.2 11.9 %copy-start.4 = (s32[8192]{0:T(1024)S(1)}, s32[8192]{0:T(1024)}, u32[]{:S(2)}) copy-start(s32[8192]{0:T(1024)} %param.13) | copy-start | bytes 98308
  31.0 6.1 %collective-permute-start.2 = (bf16[64,128,16]{1,2,0:T(8,128)(2,1)S(1)}, bf16[64,128,16]{1,2,0:T(8,128)(2,1)S(1)}, u32[]{:S(2)}, u32[]{:S(2)}) collective-permute-start(bf16[64,128,16]{1,2,0:T(8,128)(2,1)S(1)} %copy_bitcast_fusion.1), channel_id=1, source_target_pairs={{0,4},{4,8},{8,12},{12,16},{16,20},{20,24},{24,28},{28,32},{32,36}... | collective-permute-start | bytes 786440 | tf_op jit(solution)/shard_map/ppermute | solution.py:16
  35.7 4.7 %collective-permute-start.3 = (bf16[64,128,16]{1,2,0:T(8,128)(2,1)S(1)}, bf16[64,128,16]{1,2,0:T(8,128)(2,1)S(1)}, u32[]{:S(2)}, u32[]{:S(2)}) collective-permute-start(bf16[64,128,16]{1,2,0:T(8,128)(2,1)S(1)} %copy_bitcast_fusion.1), channel_id=1, source_target_pairs={{4,0},{8,4},{12,8},{16,12},{20,16},{24,20},{28,24},{32,28},{36,32}... | collective-permute-start | bytes 786440 | tf_op jit(solution)/shard_map/ppermute | solution.py:17
  47.0 47.3 %copy-start.1 = (bf16[8,3,128,128]{3,2,1,0:T(8,128)(2,1)S(1)}, bf16[8,3,128,128]{3,2,1,0:T(8,128)(2,1)}, u32[]{:S(2)}) copy-start(bf16[8,3,128,128]{3,2,1,0:T(8,128)(2,1)} %param.12) | copy-start | bytes 2359300
  94.6 8.6 %collective-permute-start.5 = (bf16[1,128,16]{1,2,0:T(8,128)(2,1)S(1)}, bf16[1,128,16]{1,2,0:T(8,128)(2,1)S(1)}, u32[]{:S(2)}, u32[]{:S(2)}) collective-permute-start(bf16[1,128,16]{1,2,0:T(8,128)(2,1)S(1)} %get-tuple-element.19), channel_id=1, source_target_pairs={{4,0},{8,4},{12,8},{16,12},{20,16},{24,20},{28,24},{32,28},{36,32}... | collective-permute-start | bytes 12296 | tf_op jit(solution)/shard_map/ppermute | solution.py:17
  95.9 8.1 %collective-permute-start.4 = (bf16[1,128,16]{1,2,0:T(8,128)(2,1)S(1)}, bf16[1,128,16]{1,2,0:T(8,128)(2,1)S(1)}, u32[]{:S(2)}, u32[]{:S(2)}) collective-permute-start(bf16[1,128,16]{1,2,0:T(8,128)(2,1)S(1)} %get-tuple-element.18), channel_id=1, source_target_pairs={{0,4},{4,8},{8,12},{12,16},{16,20},{20,24},{24,28},{28,32},{32,36}... | collective-permute-start | bytes 12296 | tf_op jit(solution)/shard_map/ppermute | solution.py:16
  104.5 5.5 %collective-permute-start.7 = (bf16[1,128,16]{1,2,0:T(8,128)(2,1)S(1)}, bf16[1,128,16]{1,2,0:T(8,128)(2,1)S(1)}, u32[]{:S(2)}, u32[]{:S(2)}) collective-permute-start(bf16[1,128,16]{1,2,0:T(8,128)(2,1)S(1)} %get-tuple-element.17), channel_id=1, source_target_pairs={{4,0},{8,4},{12,8},{16,12},{20,16},{24,20},{28,24},{32,28},{36,32}... | collective-permute-start | bytes 12296 | tf_op jit(solution)/shard_map/ppermute | solution.py:17
  105.8 5.0 %collective-permute-start.6 = (bf16[1,128,16]{1,2,0:T(8,128)(2,1)S(1)}, bf16[1,128,16]{1,2,0:T(8,128)(2,1)S(1)}, u32[]{:S(2)}, u32[]{:S(2)}) collective-permute-start(bf16[1,128,16]{1,2,0:T(8,128)(2,1)S(1)} %get-tuple-element.16), channel_id=1, source_target_pairs={{0,4},{4,8},{8,12},{12,16},{16,20},{20,24},{24,28},{28,32},{32,36}... | collective-permute-start | bytes 12296 | tf_op jit(solution)/shard_map/ppermute | solution.py:16
  118.6 68.6 %copy-start.2 = (f32[128,8192]{1,0:T(8,128)S(1)}, f32[128,8192]{1,0:T(8,128)}, u32[]{:S(2)}) copy-start(f32[128,8192]{1,0:T(8,128)} %param.15) | copy-start | bytes 12582916
  118.6 3.4 collective-permute-start.8
  193.8 1.2 collective-permute-start.9
  198.4 4.4 %collective-permute-start.11 = (bf16[1,128,16]{1,2,0:T(8,128)(2,1)S(1)}, bf16[1,128,16]{1,2,0:T(8,128)(2,1)S(1)}, u32[]{:S(2)}, u32[]{:S(2)}) collective-permute-start(bf16[1,128,16]{1,2,0:T(8,128)(2,1)S(1)} %get-tuple-element.15), channel_id=1, source_target_pairs={{4,0},{8,4},{12,8},{16,12},{20,16},{24,20},{28,24},{32,28},{36,32}... | collective-permute-start | bytes 12296 | tf_op jit(solution)/shard_map/ppermute | solution.py:17
  199.7 3.8 collective-permute-start.10
  234.8 4.8 %collective-permute-start.12 = (bf16[64,128,16]{1,2,0:T(8,128)(2,1)S(1)}, bf16[64,128,16]{1,2,0:T(8,128)(2,1)S(1)}, u32[]{:S(2)}, u32[]{:S(2)}) collective-permute-start(bf16[64,128,16]{1,2,0:T(8,128)(2,1)S(1)} %copy_bitcast_fusion), channel_id=1, source_target_pairs={{0,4},{4,8},{8,12},{12,16},{16,20},{20,24},{24,28},{28,32},{32,36}... | collective-permute-start | bytes 786440 | tf_op jit(solution)/shard_map/ppermute | solution.py:16
  238.3 5.2 %collective-permute-start.13 = (bf16[64,128,16]{1,2,0:T(8,128)(2,1)S(1)}, bf16[64,128,16]{1,2,0:T(8,128)(2,1)S(1)}, u32[]{:S(2)}, u32[]{:S(2)}) collective-permute-start(bf16[64,128,16]{1,2,0:T(8,128)(2,1)S(1)} %copy_bitcast_fusion), channel_id=1, source_target_pairs={{4,0},{8,4},{12,8},{16,12},{20,16},{24,20},{28,24},{32,28},{36,32}... | collective-permute-start | bytes 786440 | tf_op jit(solution)/shard_map/ppermute | solution.py:17
  250.3 150.8 %copy-start.3 = (f32[8192,16]{0,1:T(8,128)}, f32[8192,16]{0,1:T(8,128)S(1)}, u32[]{:S(2)}) copy-start(f32[8192,16]{0,1:T(8,128)S(1)} %fusion.7) | copy-start | bytes 1572868
Sparse Core Ops, SparseCore 0:
  239.7 28.9 all-gather.1
where the time goes:
time: 409 us; the launch traced here: 408 us
  blocking collectives  196 us (48%)
  local copies, waits for them, and re-layouts  53.3 us (13%)
  other arithmetic  52.8 us (13%)
  starting transfers between devices  35.1 us (9%)
  waiting for transfers between devices  29 us (7%)
  matrix products  27.3 us (7%)
  between operations  14.5 us (4%)
    psum x1, blocking collectives, on_device(): gram = lax.psum(partial_gram, 'rows')  131 us
    all_gather x1, blocking collectives, on_device(): lax.all_gather(coarse_rhs, 'rows', axis=0, tiled=True)  65.2 us
    scatter-add x1, other arithmetic, on_device(): jax.ops.segment_sum(fine_res, fine_local, num_segments=mid_count)  44.4 us
    gather x2, local copies, waits for them, and re-layouts, on_device(): fine_x = fine_x + mid_x[fine_local]  30.7 us
    ppermute x6, starting transfers between devices, with_halo(): before = lax.ppermute(last, axis, up)  24.4 us
    all_gather x1, waiting for transfers between devices, on_device(): lax.all_gather(basis, 'cols', axis=1, tiled=True)  18.4 us
    dot_general x3, matrix products, fine_apply(): jnp.einsum('bkij,bkjc->bic', matrix, picked, preferred_element_type=jnp.f...  17 us
  transfers between devices with their start and end apart: 15, of which 8 were waited for; matrix products, arithmetic and copies ran while one was open for 3% of the time, Pallas kernels for 0%

commit v1 on v0

--- a/solution.py
+++ b/solution.py
@@ -103,7 +103,9 @@
     )
     rounded = finished.astype(jnp.bfloat16)
     partial_gram = lax.dot_general(
-        lax.all_gather(basis, "cols", axis=1, tiled=True),
+        jnp.concatenate(
+            lax.all_to_all(jnp.stack([basis] * lax.axis_size("cols")), "cols", 0, 0), axis=1
+        ),
         rounded,
         (((0,), (0,)), ((), ())),
         preferred_element_type=jnp.float32,

time: 409 us -> 383 us (0.936)
  waiting for transfers between devices: 29 us -> 10.9 us
  between operations: 14.5 us -> 1.13 us
  starting transfers between devices: 35.1 us -> 39.8 us
    all_gather x1 -> x0, waiting for transfers between devices: 18.4 us -> none  [on_device(): lax.all_gather(basis, 'cols', axis=1, tiled=True)]
    all_to_all x0 -> x1, starting transfers between devices: none -> 4.8 us  [on_device(): lax.all_to_all(jnp.stack([basis] * lax.axis_size('cols')), 'cols', 0, 0)]
    all_to_all x0 -> x1, waiting for transfers between devices: none -> 4.17 us  [on_device(): lax.all_to_all(jnp.stack([basis] * lax.axis_size('cols')), 'cols', 0, 0)]
  transfers between devices with their start and end apart: 15 -> 15, of which waited for: 8 -> 7; matrix products, arithmetic and copies ran while one was open for 3% -> 4% of each run, Pallas kernels for 0% -> 0%
where the time goes in v1:
time: 383 us; the launch traced here: 381 us
  blocking collectives  195 us (51%)
  local copies, waits for them, and re-layouts  54.4 us (14%)
  other arithmetic  52.8 us (14%)
  starting transfers between devices  39.8 us (10%)
  matrix products  27.3 us (7%)
  waiting for transfers between devices  10.9 us (3%)
    psum x1, blocking collectives, on_device(): gram = lax.psum(partial_gram, 'rows')  130 us
    all_gather x1, blocking collectives, on_device(): lax.all_gather(coarse_rhs, 'rows', axis=0, tiled=True)  65.2 us
    scatter-add x1, other arithmetic, on_device(): jax.ops.segment_sum(fine_res, fine_local, num_segments=mid_count)  44.4 us
    gather x2, local copies, waits for them, and re-layouts, on_device(): fine_x = fine_x + mid_x[fine_local]  30.7 us
    ppermute x6, starting transfers between devices, with_halo(): before = lax.ppermute(last, axis, up)  24.4 us
    dot_general x3, matrix products, fine_apply(): jnp.einsum('bkij,bkjc->bic', matrix, picked, preferred_element_type=jnp.f...  17 us
    ppermute x6, starting transfers between devices, with_halo(): after = lax.ppermute(leading, axis, down)  7.78 us
  transfers between devices with their start and end apart: 15, of which 7 were waited for; matrix products, arithmetic and copies ran while one was open for 4% of the time, Pallas kernels for 0%

profile of v1, /device:TPU:4, one launch (start us, length us, event | category | flops | bytes accessed | tf_op | source)
XLA Modules:
  0.0 381.3 jit_solution(17093240672775462713)
XLA Ops:
  2.2 3.9 %copy.205 = bf16[64,1,128,128]{0,3,2,1:T(8,128)(2,1)} copy(bf16[64,1,128,128]{3,2,1,0:T(8,128)(2,1)S(1)} %slice-done) | data formatting | bytes 4194304
  6.1 1.9 gather_fusion
  12.5 3.1 copy.167
  18.7 5.7 %convolution_bitcast_fusion.2 = f32[64,2,8,128]{3,2,1,0:T(8,128)S(1)} fusion(bf16[64,4,128,16]{2,3,1,0:T(8,128)(2,1)S(1)} %bitcast.180, bf16[64,4,128,128]{3,2,1,0:T(8,128)(2,1)} %param.10), kind=kOutput, calls=%fused_computation.11 | convolution fusion | flops 134217728 | bytes 9961472 | tf_op jit(solution)/shard_map/bkij,bkjc->bic/dot_general | solution.py:33
  24.5 4.7 %collective-permute-start.2 = (bf16[64,128,16]{1,2,0:T(8,128)(2,1)S(1)}, bf16[64,128,16]{1,2,0:T(8,128)(2,1)S(1)}, u32[]{:S(2)}, u32[]{:S(2)}) collective-permute-start(bf16[64,128,16]{1,2,0:T(8,128)(2,1)S(1)} %copy_bitcast_fusion.1), channel_id=1, source_target_pairs={{0,4},{4,8},{8,12},{12,16},{16,20},{20,24},{24,28},{28,32},{32,36}... | collective-permute-start | bytes 786440 | tf_op jit(solution)/shard_map/ppermute | solution.py:16
  30.6 3.3 collective-permute-done.3
  34.8 5.7 %convolution_bitcast_fusion.1 = f32[64,2,8,128]{3,2,1,0:T(8,128)S(1)} fusion(bf16[64,4,128,16]{2,3,1,0:T(8,128)(2,1)S(1)} %bitcast.181, bf16[64,4,128,128]{3,2,1,0:T(8,128)(2,1)} %param.10), kind=kOutput, calls=%fused_computation.10 | convolution fusion | flops 134217728 | bytes 9961472 | tf_op jit(solution)/shard_map/bkij,bkjc->bic/dot_general | solution.py:33
  40.5 2.6 copy.173
  43.2 44.4 %scatter_custom_fusion = f32[1024,16]{1,0:T(8,128)S(1)} fusion(s32[8192]{0:T(1024)S(1)} %get-tuple-element.11, f32[8192,16]{1,0:T(8,128)} %copy.173, f32[]{:T(128)} %constant.25.clone.1), kind=kCustom, calls=%fused_computation.51 | custom fusion | flops 131072 | bytes 66048 | tf_op jit(solution)/shard_map/scatter-add | solution.py:77
  89.4 7.3 %collective-permute-start.4 = (bf16[1,128,16]{1,2,0:T(8,128)(2,1)S(1)}, bf16[1,128,16]{1,2,0:T(8,128)(2,1)S(1)}, u32[]{:S(2)}, u32[]{:S(2)}) collective-permute-start(bf16[1,128,16]{1,2,0:T(8,128)(2,1)S(1)} %get-tuple-element.18), channel_id=1, source_target_pairs={{0,4},{4,8},{8,12},{12,16},{16,20},{20,24},{24,28},{28,32},{32,36}... | collective-permute-start | bytes 12296 | tf_op jit(solution)/shard_map/ppermute | solution.py:16
  99.3 4.2 %collective-permute-start.6 = (bf16[1,128,16]{1,2,0:T(8,128)(2,1)S(1)}, bf16[1,128,16]{1,2,0:T(8,128)(2,1)S(1)}, u32[]{:S(2)}, u32[]{:S(2)}) collective-permute-start(bf16[1,128,16]{1,2,0:T(8,128)(2,1)S(1)} %get-tuple-element.16), channel_id=1, source_target_pairs={{0,4},{4,8},{8,12},{12,16},{16,20},{20,24},{24,28},{28,32},{32,36}... | collective-permute-start | bytes 12296 | tf_op jit(solution)/shard_map/ppermute | solution.py:16
  105.6 6.4 %scatter_custom_fusion.1 = f32[256,16]{1,0:T(8,128)S(1)} fusion(s32[1024]{0:T(1024)S(1)} %get-tuple-element.13, f32[1024,16]{1,0:T(8,128)} %bitcast_subtract_fusion.3, f32[]{:T(128)} %constant.25.clone.1), kind=kCustom, calls=%fused_computation.70 | custom fusion | flops 16384 | bytes 16896 | tf_op jit(solution)/shard_map/scatter-add | solution.py:81
  112.1 2.5 collective-permute-start.8
  115.5 65.2 %all_gather.3 = f32[8192,16]{1,0:T(8,128)S(1)} all-gather(f32[128,16]{1,0:T(8,128)S(1)} %select_add_fusion), channel_id=1, replica_groups=mesh['rows'=64,'cols'=4] {'rows'}, dimensions={0}, use_global_device_ids=true | all-gather | bytes 532480 | tf_op jit(solution)/shard_map/all_gather | solution.py:88
  180.7 6.6 %convolution_bitcast_fusion.4 = f32[128,16]{0,1:T(8,128)S(1)} fusion(f32[8192,16]{1,0:T(8,128)S(1)} %all_gather.3, f32[128,8192]{1,0:T(8,128)S(1)} %copy-done.2), kind=kOutput, calls=%fused_computation.22 | convolution fusion | flops 201326592 | bytes 4726784 | tf_op jit(solution)/shard_map/dot_general | solution.py:86
  188.6 2.8 gather_fusion.4
  193.2 3.0 collective-permute-start.10
  197.5 27.9 %gather_fusion.5 = f32[8192,16]{1,0:T(8,128)} fusion(f32[1024,16]{1,0:T(8,128)S(1)} %copy.194, s32[8192]{0:T(1024)S(1)} %get-tuple-element.10), kind=kCustom, calls=%fused_computation.5 | custom fusion | bytes 1081344 | tf_op jit(solution)/shard_map/gather | solution.py:100
  225.4 2.8 copy.195
  228.4 3.4 collective-permute-start.12
  234.1 4.8 %all-to-all-start = ((bf16[4,8192,16]{1,2,0:T(8,128)(2,1)}), bf16[4,8192,16]{1,2,0:T(8,128)(2,1)}, u32[]{:S(2)}, u32[]{:S(2)}) async-start(bf16[4,8192,16]{1,2,0:T(8,128)(2,1)} %stack.2), calls=%async_computation | async-start | bytes 2097152 | tf_op jit(solution)/shard_map/all_to_all | solution.py:107
  239.9 5.7 %convolution_bitcast_fusion = f32[64,2,8,128]{3,2,1,0:T(8,128)S(1)} fusion(bf16[64,4,128,16]{2,3,1,0:T(8,128)(2,1)S(1)} %bitcast.179, bf16[64,4,128,128]{3,2,1,0:T(8,128)(2,1)} %param.10), kind=kOutput, calls=%fused_computation.9 | convolution fusion | flops 134217728 | bytes 9961472 | tf_op jit(solution)/shard_map/bkij,bkjc->bic/dot_general | solution.py:33
  245.8 4.2 %all-to-all-done = bf16[4,8192,16]{1,2,0:T(8,128)(2,1)} async-done(((bf16[4,8192,16]{1,2,0:T(8,128)(2,1)}), bf16[4,8192,16]{1,2,0:T(8,128)(2,1)}, u32[]{:S(2)}, u32[]{:S(2)}) %all-to-all-start) | async-done | bytes 1048608 | tf_op jit(solution)/shard_map/all_to_all | solution.py:107
  251.5 129.7 %psum.7 = f32[64,16]{0,1:T(8,128)} all-reduce(f32[64,16]{0,1:T(8,128)S(1)} %convolution_bitcast_fusion.3), channel_id=1, replica_groups=mesh['rows'=64,'cols'=4] {'rows'}, use_global_device_ids=true, to_apply=%region_2.3 | all-reduce | flops 1024 | bytes 8192 | tf_op jit(solution)/shard_map/psum | solution.py:113
  (93 shorter events, 28.2 us)
Async XLA Ops:
  0.6 1.6 slice-start
  2.2 6.0 %copy-start = (f32[8192,16]{0,1:T(8,128)S(1)}, f32[8192,16]{0,1:T(8,128)}, u32[]{:S(2)}) copy-start(f32[8192,16]{0,1:T(8,128)} %param.8) | copy-start | bytes 1572868
  2.2 9.1 %copy-start.7 = (s32[64,4]{0,1:T(4,128)S(1)}, s32[64,4]{0,1:T(4,128)}, u32[]{:S(2)}) copy-start(s32[64,4]{0,1:T(4,128)} %param.11) | copy-start | bytes 3076
  6.1 11.5 %copy-start.6 = (s32[1024]{0:T(1024)S(1)}, s32[1024]{0:T(1024)}, u32[]{:S(2)}) copy-start(s32[1024]{0:T(1024)} %param.14) | copy-start | bytes 12292
  8.2 9.4 %collective-permute-start = (bf16[64,128,16]{1,2,0:T(8,128)(2,1)S(1)}, bf16[64,128,16]{1,2,0:T(8,128)(2,1)S(1)}, u32[]{:S(2)}, u32[]{:S(2)}) collective-permute-start(bf16[64,128,16]{1,2,0:T(8,128)(2,1)S(1)} %copy_bitcast_fusion.2), channel_id=1, source_target_pairs={{0,4},{4,8},{8,12},{12,16},{16,20},{20,24},{24,28},{28,32},{32,36}... | collective-permute-start | bytes 786440 | tf_op jit(solution)/shard_map/ppermute | solution.py:16
  10.0 7.7 %collective-permute-start.1 = (bf16[64,128,16]{1,2,0:T(8,128)(2,1)S(1)}, bf16[64,128,16]{1,2,0:T(8,128)(2,1)S(1)}, u32[]{:S(2)}, u32[]{:S(2)}) collective-permute-start(bf16[64,128,16]{1,2,0:T(8,128)(2,1)S(1)} %copy_bitcast_fusion.2), channel_id=1, source_target_pairs={{4,0},{8,4},{12,8},{16,12},{20,16},{24,20},{28,24},{32,28},{36,32}... | collective-permute-start | bytes 786440 | tf_op jit(solution)/shard_map/ppermute | solution.py:17
  18.7 11.9 %copy-start.5 = (s32[8192]{0:T(1024)S(1)}, s32[8192]{0:T(1024)}, u32[]{:S(2)}) copy-start(s32[8192]{0:T(1024)} %param.13) | copy-start | bytes 98308
  24.5 6.1 %collective-permute-start.2 = (bf16[64,128,16]{1,2,0:T(8,128)(2,1)S(1)}, bf16[64,128,16]{1,2,0:T(8,128)(2,1)S(1)}, u32[]{:S(2)}, u32[]{:S(2)}) collective-permute-start(bf16[64,128,16]{1,2,0:T(8,128)(2,1)S(1)} %copy_bitcast_fusion.1), channel_id=1, source_target_pairs={{0,4},{4,8},{8,12},{12,16},{16,20},{20,24},{24,28},{28,32},{32,36}... | collective-permute-start | bytes 786440 | tf_op jit(solution)/shard_map/ppermute | solution.py:16
  29.2 4.7 %collective-permute-start.3 = (bf16[64,128,16]{1,2,0:T(8,128)(2,1)S(1)}, bf16[64,128,16]{1,2,0:T(8,128)(2,1)S(1)}, u32[]{:S(2)}, u32[]{:S(2)}) collective-permute-start(bf16[64,128,16]{1,2,0:T(8,128)(2,1)S(1)} %copy_bitcast_fusion.1), channel_id=1, source_target_pairs={{4,0},{8,4},{12,8},{16,12},{20,16},{24,20},{28,24},{32,28},{36,32}... | collective-permute-start | bytes 786440 | tf_op jit(solution)/shard_map/ppermute | solution.py:17
  40.5 47.3 %copy-start.1 = (bf16[8,3,128,128]{3,2,1,0:T(8,128)(2,1)S(1)}, bf16[8,3,128,128]{3,2,1,0:T(8,128)(2,1)}, u32[]{:S(2)}) copy-start(bf16[8,3,128,128]{3,2,1,0:T(8,128)(2,1)} %param.12) | copy-start | bytes 2359300
  88.0 8.6 %collective-permute-start.5 = (bf16[1,128,16]{1,2,0:T(8,128)(2,1)S(1)}, bf16[1,128,16]{1,2,0:T(8,128)(2,1)S(1)}, u32[]{:S(2)}, u32[]{:S(2)}) collective-permute-start(bf16[1,128,16]{1,2,0:T(8,128)(2,1)S(1)} %get-tuple-element.19), channel_id=1, source_target_pairs={{4,0},{8,4},{12,8},{16,12},{20,16},{24,20},{28,24},{32,28},{36,32}... | collective-permute-start | bytes 12296 | tf_op jit(solution)/shard_map/ppermute | solution.py:17
  89.4 8.1 %collective-permute-start.4 = (bf16[1,128,16]{1,2,0:T(8,128)(2,1)S(1)}, bf16[1,128,16]{1,2,0:T(8,128)(2,1)S(1)}, u32[]{:S(2)}, u32[]{:S(2)}) collective-permute-start(bf16[1,128,16]{1,2,0:T(8,128)(2,1)S(1)} %get-tuple-element.18), channel_id=1, source_target_pairs={{0,4},{4,8},{8,12},{12,16},{16,20},{20,24},{24,28},{28,32},{32,36}... | collective-permute-start | bytes 12296 | tf_op jit(solution)/shard_map/ppermute | solution.py:16
  98.0 5.5 %collective-permute-start.7 = (bf16[1,128,16]{1,2,0:T(8,128)(2,1)S(1)}, bf16[1,128,16]{1,2,0:T(8,128)(2,1)S(1)}, u32[]{:S(2)}, u32[]{:S(2)}) collective-permute-start(bf16[1,128,16]{1,2,0:T(8,128)(2,1)S(1)} %get-tuple-element.17), channel_id=1, source_target_pairs={{4,0},{8,4},{12,8},{16,12},{20,16},{24,20},{28,24},{32,28},{36,32}... | collective-permute-start | bytes 12296 | tf_op jit(solution)/shard_map/ppermute | solution.py:17
  99.3 5.0 %collective-permute-start.6 = (bf16[1,128,16]{1,2,0:T(8,128)(2,1)S(1)}, bf16[1,128,16]{1,2,0:T(8,128)(2,1)S(1)}, u32[]{:S(2)}, u32[]{:S(2)}) collective-permute-start(bf16[1,128,16]{1,2,0:T(8,128)(2,1)S(1)} %get-tuple-element.16), channel_id=1, source_target_pairs={{0,4},{4,8},{8,12},{12,16},{16,20},{20,24},{24,28},{28,32},{32,36}... | collective-permute-start | bytes 12296 | tf_op jit(solution)/shard_map/ppermute | solution.py:16
  112.1 68.6 %copy-start.2 = (f32[128,8192]{1,0:T(8,128)S(1)}, f32[128,8192]{1,0:T(8,128)}, u32[]{:S(2)}) copy-start(f32[128,8192]{1,0:T(8,128)} %param.15) | copy-start | bytes 12582916
  112.1 3.4 collective-permute-start.8
  187.3 1.2 collective-permute-start.9
  191.9 4.4 %collective-permute-start.11 = (bf16[1,128,16]{1,2,0:T(8,128)(2,1)S(1)}, bf16[1,128,16]{1,2,0:T(8,128)(2,1)S(1)}, u32[]{:S(2)}, u32[]{:S(2)}) collective-permute-start(bf16[1,128,16]{1,2,0:T(8,128)(2,1)S(1)} %get-tuple-element.15), channel_id=1, source_target_pairs={{4,0},{8,4},{12,8},{16,12},{20,16},{24,20},{28,24},{32,28},{36,32}... | collective-permute-start | bytes 12296 | tf_op jit(solution)/shard_map/ppermute | solution.py:17
  193.2 3.8 %collective-permute-start.10 = (bf16[1,128,16]{1,2,0:T(8,128)(2,1)S(1)}, bf16[1,128,16]{1,2,0:T(8,128)(2,1)S(1)}, u32[]{:S(2)}, u32[]{:S(2)}) collective-permute-start(bf16[1,128,16]{1,2,0:T(8,128)(2,1)S(1)} %get-tuple-element.14), channel_id=1, source_target_pairs={{0,4},{4,8},{8,12},{12,16},{16,20},{20,24},{24,28},{28,32},{32,36}... | collective-permute-start | bytes 12296 | tf_op jit(solution)/shard_map/ppermute | solution.py:16
  225.4 7.7 %copy-start.4 = (bf16[8192,16]{0,1:T(8,128)(2,1)S(1)}, bf16[8192,16]{0,1:T(8,128)(2,1)}, u32[]{:S(2)}) copy-start(bf16[8192,16]{0,1:T(8,128)(2,1)} %param.9) | copy-start | bytes 786436
  228.4 10.6 %collective-permute-start.12 = (bf16[64,128,16]{1,2,0:T(8,128)(2,1)S(1)}, bf16[64,128,16]{1,2,0:T(8,128)(2,1)S(1)}, u32[]{:S(2)}, u32[]{:S(2)}) collective-permute-start(bf16[64,128,16]{1,2,0:T(8,128)(2,1)S(1)} %copy_bitcast_fusion), channel_id=1, source_target_pairs={{0,4},{4,8},{8,12},{12,16},{16,20},{20,24},{24,28},{28,32},{32,36}... | collective-permute-start | bytes 786440 | tf_op jit(solution)/shard_map/ppermute | solution.py:16
  231.8 7.2 %collective-permute-start.13 = (bf16[64,128,16]{1,2,0:T(8,128)(2,1)S(1)}, bf16[64,128,16]{1,2,0:T(8,128)(2,1)S(1)}, u32[]{:S(2)}, u32[]{:S(2)}) collective-permute-start(bf16[64,128,16]{1,2,0:T(8,128)(2,1)S(1)} %copy_bitcast_fusion), channel_id=1, source_target_pairs={{4,0},{8,4},{12,8},{16,12},{20,16},{24,20},{28,24},{32,28},{36,32}... | collective-permute-start | bytes 786440 | tf_op jit(solution)/shard_map/ppermute | solution.py:17
  234.1 15.8 %all-to-all-start = ((bf16[4,8192,16]{1,2,0:T(8,128)(2,1)}), bf16[4,8192,16]{1,2,0:T(8,128)(2,1)}, u32[]{:S(2)}, u32[]{:S(2)}) async-start(bf16[4,8192,16]{1,2,0:T(8,128)(2,1)} %stack.2), calls=%async_computation | async-start | bytes 2097152 | tf_op jit(solution)/shard_map/all_to_all | solution.py:107
  245.8 135.5 %copy-start.3 = (f32[8192,16]{0,1:T(8,128)}, f32[8192,16]{0,1:T(8,128)S(1)}, u32[]{:S(2)}) copy-start(f32[8192,16]{0,1:T(8,128)S(1)} %fusion.7) | copy-start | bytes 1572868
